TPU v7x, 1024 devices: a whole 8x8x8 slice. The times are simulated.
1024 devices in a mesh: row: 16 (over z, core), col: 64 (over x, y).
Axes of the slice: x: 8, y: 8, z: 8, core: 2. Of those that a mesh axis runs over, the one named last changes fastest.
Arguments:
- matrix: float32 [12288, 24576], P('row', 'col'), may hold values from -6 to 6
- panel_t: float32 [512, 12288], P('col', 'row'), may hold values from -0.25 to 0.25
- inverse_lower: float32 [512, 512], replicated, as said below
- pivot_rows: int32 [512], replicated, may hold values from 0 to 12287, as said below
Outputs:
- updated: float32 [12288, 24576], P('row', 'col')
Inputs may be any that keep to these rules, and one draw needn't show every extreme that they name: `pivot_rows`: entries are distinct; entry j is either j itself or a row at or past 768, so the interchanges are disjoint swaps. Exactly 256 entries differ from their position. The rows of one index of row are named by at most 32 entries, and in every draw some index of row is named by exactly 32. `inverse_lower`: zero above the diagonal and one on it.
All inputs are finite; a program needn't handle non-finite values.
Results may differ from a plain program's by a relative error of at most 0.000058.
Values sent between devices are 32-bit elements; how exact they have to be, the bound alone decides.
A program may use at most 32 MiB of HBM per device.

v0:
```python
import jax
import jax.numpy as jnp
from jax import lax
from jax.sharding import PartitionSpec as P


def from_root(value, axis, source):
    kept = jnp.where(lax.axis_index(axis) == source, value, 0).astype(value.dtype)
    return lax.psum(kept, axis)


def local(matrix, panel_t, inverse_lower, pivot_rows):
    rows, cols = matrix.shape
    width = inverse_lower.shape[0]
    first = lax.axis_index("row") * rows
    places = jnp.arange(width, dtype=jnp.int32)
    local_src = pivot_rows - first
    inside = (local_src >= 0) & (local_src < rows)
    fetched = jnp.take(matrix, jnp.clip(local_src, 0, rows - 1), axis=0)
    picked = jnp.where(inside[:, None], fetched, jnp.zeros_like(fetched))
    initial = from_root(matrix[:width], "row", 0)
    target = jnp.where(inside & (pivot_rows != places), local_src, rows)
    swapped = matrix.at[target].set(initial, mode="drop")
    stacked = lax.psum(picked, "row")
    upper = jnp.dot(
        inverse_lower, stacked, precision=lax.Precision.HIGHEST, preferred_element_type=jnp.float32
    )
    product = lax.dot_general(
        lax.all_gather(panel_t, "col", axis=0, tiled=True),
        upper,
        (((0,), (0,)), ((), ())),
        precision=lax.Precision.HIGHEST,
        preferred_element_type=jnp.float32,
    )
    updated = swapped - product
    head = jnp.where(first == 0, upper, updated[:width])
    updated = lax.dynamic_update_slice_in_dim(updated, head, 0, 0)
    return updated


def solution(mesh):
    in_specs = (P("row", "col"), P("col", "row"), P(), P())
    out_specs = P("row", "col")
    return jax.shard_map(local, mesh=mesh, in_specs=in_specs, out_specs=out_specs, check_vma=False)
```

profile of v0, /device:TPU:1, one launch (start us, length us, event | category | flops | bytes accessed | tf_op | source)
XLA Modules:
  0.0 172.6 jit_solution(16677101474568702908)
XLA Ops:
  7.4 0.0 copy-start
  7.4 0.0 copy-start.2
  7.4 0.0 all-reduce.3.cloned.1.call-start
  7.4 1.4 copy.12
  8.7 0.0 copy-done.2
  8.8 1.6 gather_fusion
  10.4 1.4 select_select_fusion
  11.7 0.0 all-reduce.3.cloned.1.call-update
  11.8 0.0 all-gather.2.cloned.1.call-start
  11.8 0.5 all-gather.2.cloned.1.call-update
  12.4 140.0 %all-reduce.3.cloned.1.call-done = (f32[512,384]{1,0:T(8,128)}, f32[512,384]{1,0:T(8,128)}) async-done(((f32[512,384]{1,0:T(8,128)}, f32[512,384]{1,0:T(8,128)}), (f32[512,384]{1,0:T(8,128)}, f32[512,384]{1,0:T(8,128)})) %all-reduce.3.cloned.1.call-update) | async-done | bytes 1572880 | tf_op jit(solution)/shard_map/psum | solution.py:9
  152.3 3.3 %scatter_fusion = f32[768,384]{1,0:T(8,128)S(1)} fusion(f32[768,384]{1,0:T(8,128)S(1)} %copy.12, s32[512]{0:T(512)S(1)} %compare_select_fusion.1, f32[512,384]{1,0:T(8,128)} %get-tuple-element.5), kind=kCustom, calls=%fused_computation.1 | custom fusion | bytes 2361344 | tf_op jit(solution)/shard_map/scatter | solution.py:23
  155.6 0.0 copy-start.1
  155.6 1.4 copy.5
  157.0 0.0 copy-done
  157.0 0.0 copy-done.1
  157.0 2.7 %fusion.3 = f32[384,512]{1,0:T(8,128)S(1)} fusion(f32[512,384]{1,0:T(8,128)S(1)} %copy-done.1, f32[512,512]{1,0:T(8,128)S(1)} %copy-done), kind=kOutput, calls=%fused_computation.15 | convolution fusion | flops 1207959552 | bytes 2621440 | tf_op jit(solution)/shard_map/dot_general | solution.py:25
  159.7 0.0 all-gather.2.cloned.1.call-done
  159.7 3.8 %fusion = f32[768,384]{0,1:T(8,128)S(1)} fusion(f32[768,384]{0,1:T(8,128)} %copy.5, f32[384,512]{1,0:T(8,128)S(1)} %fusion.3, f32[512,768]{1,0:T(8,128)} %all-gather.2.cloned.1.call-done), kind=kOutput, calls=%fused_computation.3 | convolution fusion | flops 1812234240 | bytes 4718592 | tf_op jit(solution)/shard_map/dot_general | solution.py:28
  163.6 0.2 fusion.1
  163.8 1.4 copy.6
  (3 shorter events, 0.0 us)
Async XLA Ops:
  7.4 149.6 %copy-start = (f32[512,512]{1,0:T(8,128)S(1)}, f32[512,512]{1,0:T(8,128)}, u32[]{:S(2)}) copy-start(f32[512,512]{1,0:T(8,128)} %param.6) | copy-start | bytes 3145732
  7.4 1.4 copy-start.2
  7.4 145.0 %all-reduce.3.cloned.1.call-start = ((), (), s32[]{:S(2)}) async-start(), calls=%async_computation.1 | async-start | bytes 3145728 | tf_op jit(solution)/shard_map/psum | solution.py:9
  11.8 147.9 %all-gather.2.cloned.1.call-start = ((), (), s32[]{:S(2)}) async-start(), calls=%async_computation | async-start | bytes 1597440 | tf_op jit(solution)/shard_map/all_gather | solution.py:29
  155.6 1.4 copy-start.1
Sparse Core Ops, SparseCore 0:
  11.9 140.4 all-reduce.2
Sparse Core Ops, SparseCore 1:
  16.5 95.2 all-gather.1
where the time goes:
time: 173 us
  waiting for transfers between devices  141 us (82%)
  between operations  14.9 us (9%)
  local copies, waits for them, and re-layouts  9.01 us (5%)
  matrix products  6.5 us (4%)
    psum x1, waiting for transfers between devices, from_root(): return lax.psum(kept, axis)  140 us
    scatter x2, local copies, waits for them, and re-layouts, local(): swapped = matrix.at[target].set(initial, mode='drop')  4.65 us
    dot_general x1, matrix products, local(): lax.dot_general(lax.all_gather(panel_t, 'col', axis=0, tiled=True), upper...  3.84 us
  transfers between devices with their start and end apart: 2, of which 1 were waited for; matrix products, arithmetic and copies ran while one was open for 4% of the time, Pallas kernels for 0%

commit v1 on v0

v1 whole, which is shorter than its diff:
```python
import functools

import jax
import jax.numpy as jnp
from jax import lax
from jax.experimental import pallas as pl
from jax.experimental.pallas import tpu as pltpu
from jax.sharding import PartitionSpec as P

MESH = pl.DeviceIdType.MESH
F32, BF16 = jnp.float32, jnp.bfloat16

NX, NY, NZ = 8, 8, 8
SLOTS = 32
CHUNKS = 4


def order_of(n):
    order = [0]
    for d in range(1, n // 2 + 1):
        order.append(d)
        if d <= (n - 1) // 2:
            order.append(-d)
    return order


def groups_of(n):
    order = order_of(n)
    top = n // 2
    groups = [(0, 1, 0)]
    d = 1
    while d <= top:
        last = top if (d + 1 == top and n % 2 == 0) else d
        slots = [i for i, o in enumerate(order) if d <= abs(o) <= last]
        groups.append((slots[0], len(slots), last))
        d = last + 1
    return groups


def split2(v):
    hi = v.astype(BF16)
    return hi, (v - hi.astype(F32)).astype(BF16)


def split3(v):
    hi = v.astype(BF16)
    rest = v - hi.astype(F32)
    mid = rest.astype(BF16)
    return hi, mid, (rest - mid.astype(F32)).astype(BF16)


def dot(a, b):
    return jnp.dot(a, b, preferred_element_type=F32)


def dot_t(a, b):
    return lax.dot_general(a, b, (((0,), (0,)), ((), ())), preferred_element_type=F32)


def select(onehot, v):
    hi, mid, lo = split3(v)
    return dot(onehot, hi) + dot(onehot, mid) + dot(onehot, lo)


def lane_iota(shape):
    return lax.broadcasted_iota(jnp.int32, shape, 1).astype(F32)


def sub_iota(shape):
    return lax.broadcasted_iota(jnp.int32, shape, 0).astype(F32)


def onehot(test):
    return jnp.where(test, 1.0, 0.0)


def kernel(
    mat_any, pan_any, inv_any, piv_ref, out_any,
    mat, inv, inv_rel, buf_a, buf_b, work, init, lpe_hi, lpe_lo, up_a, up_b,
    local_sem, send_a, send_b, a1, a2, b1, b2,
    zs, zr, zps, zpr, us, ur, ups, upr, ims, imr, ifs, ifr, out_sem,
):
    rows, cols = mat.shape
    width = inv.shape[0]
    half_rows = rows // 2
    free = width // 2
    n_row = 2 * NZ
    cls_rows = free // 2
    chunk = cls_rows // CHUNKS
    row, col = lax.axis_index("row"), lax.axis_index("col")
    z, core = row // 2, row % 2
    x, y = col // NY, col % NY
    s = 1 - 2 * core

    def at_x(d):
        return (row, lax.rem(x + d + 2 * NX, NX) * NY + y)

    def at_y(d):
        return (row, x * NY + lax.rem(y + d + 2 * NY, NY))

    def at_z(d):
        return (lax.rem(z + d + 2 * NZ, NZ) * 2 + core, col)

    partner = (z * 2 + 1 - core, col)

    barrier = pltpu.get_barrier_semaphore()
    for other in (at_x(1), at_x(-1), at_y(1), at_y(-1), at_z(1), at_z(-1), partner):
        pl.semaphore_signal(barrier, inc=1, device_id=other, device_id_type=MESH)

    half = pan_any.shape[1] // 2
    loads = [
        pltpu.make_async_copy(mat_any, mat, local_sem.at[0]),
        pltpu.make_async_copy(pan_any.at[:, 0:half], buf_a.at[0:8], local_sem.at[1]),
        pltpu.make_async_copy(pan_any.at[:, half:], buf_b.at[0:8], local_sem.at[2]),
        pltpu.make_async_copy(inv_any, inv, local_sem.at[3]),
    ]
    for load in loads:
        load.start()

    p = piv_ref[...].astype(F32)
    place = lane_iota(p.shape)
    moved = p != place
    owner = jnp.floor((p + 0.5) * (1.0 / rows))
    local_row = p - owner * rows
    cls = jnp.where(moved, owner, 0.0)
    member = onehot(jnp.broadcast_to(cls, (n_row, width)) == sub_iota((n_row, width)))
    before = onehot(sub_iota((width, width)) < lane_iota((width, width))).astype(BF16)
    counts = dot(member.astype(BF16), before)
    rank = jnp.sum(member * counts, axis=0, keepdims=True)
    g = jnp.where(moved, free + SLOTS * owner + rank, rank)

    mine = onehot(
        jnp.broadcast_to(g, (SLOTS, width))
        == sub_iota((SLOTS, width)) + (free + SLOTS * row).astype(F32)
    )
    spot = jnp.sum(mine * local_row, axis=1, keepdims=True)
    used = jnp.sum(mine, axis=1, keepdims=True)
    spot = jnp.where(used > 0.0, spot, -1.0)
    pick = onehot(jnp.broadcast_to(spot, (SLOTS, rows)) == lane_iota((SLOTS, rows))).astype(BF16)

    own_slots = pl.ds(pl.multiple_of(free + SLOTS * row, SLOTS), SLOTS)
    loads[0].wait()
    work[own_slots, :] = select(pick, mat[...])

    is_root = row == 0

    @pl.when(is_root)
    def _():
        head = mat[0:width, :]
        unmoved = onehot(jnp.broadcast_to(g, (free, width)) == sub_iota((free, width))).astype(BF16)
        work[0:free, :] = select(unmoved, head)
        owner_z = jnp.floor((owner + 0.5) * 0.5)
        owner_c = owner - 2.0 * owner_z
        reach = jnp.where(owner_c == 0.0, owner_z, NZ - owner_z)
        reach = jnp.where(reach >= NZ, 0.0, reach)
        goal = jnp.where(moved, (owner_c * NZ + reach) * SLOTS + rank, -1.0)
        total = n_row * SLOTS
        send_to = onehot(jnp.broadcast_to(goal, (total, width)) == sub_iota((total, width))).astype(BF16)
        init[...] = select(send_to, head)

    for load in loads[1:]:
        load.wait()
    pl.semaphore_wait(barrier, 7)

    def send(src, dst, ss, rs, to):
        c = pltpu.make_async_remote_copy(
            src_ref=src, dst_ref=dst, send_sem=ss, recv_sem=rs, device_id=to, device_id_type=MESH
        )
        c.start()
        return c

    def recv(ref, sem):
        pltpu.make_async_copy(ref, ref, sem).wait()

    ox, oy, oz = order_of(NX), order_of(NY), order_of(NZ)

    class Half:
        def __init__(self, buf, first, second, n_in, n_out, at_in, at_out, send_sem):
            self.buf, self.first, self.second = buf, first, second
            self.n_in, self.n_out = n_in, n_out
            self.at_in, self.at_out = at_in, at_out
            self.o_in, self.o_out = order_of(n_in), order_of(n_out)
            self.groups = groups_of(n_in)
            self.send_sem = send_sem

        def span(self, o, i0, n):
            base = (self.o_out.index(o) * self.n_in + i0) * 8
            return self.buf.at[base:base + n * 8]

        def next_ones(self, d, n):
            out = []
            if 0 <= d < n // 2:
                out.append(d + 1)
            if 0 >= d > -((n - 1) // 2):
                out.append(d - 1)
            return out

        def inner_from(self, d):
            i = self.o_in.index(d)
            for t in self.next_ones(d, self.n_in):
                j = self.o_in.index(t)
                step = 1 if t > 0 else -1
                send(self.span(0, i, 1), self.span(0, j, 1), self.send_sem, self.first.at[j], self.at_in(step * s))

        def outer_from(self, o, k):
            i0, n, _ = self.groups[k]
            for t in self.next_ones(o, self.n_out):
                step = 1 if t > 0 else -1
                send(
                    self.span(o, i0, n), self.span(t, i0, n), self.send_sem,
                    self.second.at[self.o_out.index(t), k], self.at_out(step * s),
                )

        def inner_round(self, h):
            for d in (h, -h):
                if d in self.o_in:
                    i = self.o_in.index(d)
                    recv(self.span(0, i, 1), self.first.at[i])
                    self.inner_from(d)
            for k, (_, _, hops) in enumerate(self.groups):
                if hops == h:
                    self.outer_from(0, k)

        def outer_round(self, h):
            for k, (i0, n, hops) in enumerate(self.groups):
                for o in (h - hops, hops - h):
                    if o != 0 and h > hops and o in self.o_out:
                        recv(self.span(o, i0, n), self.second.at[self.o_out.index(o), k])
                        self.outer_from(o, k)

        def finish(self):
            ref = self.buf.at[0:(self.n_in * self.n_out - 1) * 8]
            pltpu.make_async_copy(ref, ref, self.send_sem).wait()

    half_a = Half(buf_a, a1, a2, NY, NX, at_y, at_x, send_a.at[0])
    half_b = Half(buf_b, b1, b2, NX, NY, at_x, at_y, send_b.at[0])
    for h in (half_a, half_b):
        h.outer_from(0, 0)
        h.inner_from(0)

    fwd, bwd = NZ // 2, (NZ - 1) // 2

    def slot_rows(d):
        src = lax.rem(z - s * d + 2 * NZ, NZ) * 2 + core
        return work.at[pl.ds(pl.multiple_of(free + SLOTS * src, SLOTS), SLOTS)]

    def partner_rows(d):
        src = lax.rem(z + s * d + 2 * NZ, NZ) * 2 + 1 - core
        return work.at[pl.ds(pl.multiple_of(free + SLOTS * src, SLOTS), SLOTS)]

    z_sends = []

    def slots_from(d):
        ref = slot_rows(d)
        if 0 <= d < fwd:
            j = oz.index(d + 1)
            z_sends.append(send(ref, ref, zs.at[j], zr.at[j], at_z(s)))
        if 0 >= d > -bwd:
            j = oz.index(d - 1)
            z_sends.append(send(ref, ref, zs.at[j], zr.at[j], at_z(-s)))
        i = oz.index(d)
        z_sends.append(send(ref, ref, zps.at[i], zpr.at[i], partner))

    df = lax.rem(s * z + NZ, NZ)
    on_fwd = df <= fwd
    dist = jnp.where(on_fwd, df, NZ - df)
    is_second = (z == 0) & (core == 1)
    source = z == 0
    relays_u = jnp.logical_not(source) & (((df < fwd) & on_fwd) | (jnp.logical_not(on_fwd) & (dist < bwd)))
    ahead = jnp.where(on_fwd, s, -s)

    def u_rows(c, k):
        return work.at[pl.ds(pl.multiple_of(c * cls_rows + k * chunk, chunk), chunk)]

    def u_copy(ref, way, slot, k):
        return pltpu.make_async_remote_copy(
            src_ref=ref, dst_ref=ref, send_sem=us.at[slot, k], recv_sem=ur.at[k],
            device_id=at_z(way), device_id_type=MESH,
        )

    def u_partner(ref, k):
        return pltpu.make_async_remote_copy(
            src_ref=ref, dst_ref=ref, send_sem=ups.at[k], recv_sem=upr.at[k],
            device_id=partner, device_id_type=MESH,
        )

    def u_second(k):
        ref = u_rows(1, k)
        return pltpu.make_async_remote_copy(
            src_ref=ref, dst_ref=ref, send_sem=us.at[2, k], recv_sem=ur.at[k],
            device_id=partner, device_id_type=MESH,
        )

    def i_rows(c, q):
        return init.at[pl.ds(pl.multiple_of((c * NZ + q) * SLOTS, SLOTS), SLOTS)]

    def i_copy(q, way):
        ref = i_rows(core, q)
        return pltpu.make_async_remote_copy(
            src_ref=ref, dst_ref=ref, send_sem=ifs.at[q], recv_sem=ifr.at[q],
            device_id=at_z(way), device_id_type=MESH,
        )

    def i_second():
        ref = init.at[NZ * SLOTS:2 * NZ * SLOTS]
        return pltpu.make_async_remote_copy(
            src_ref=ref, dst_ref=ref, send_sem=ims.at[0], recv_sem=imr.at[0],
            device_id=partner, device_id_type=MESH,
        )

    def i_source_sends(act):
        for q in sorted(range(1, NZ), key=lambda v: -min(v, NZ - v)):
            act(i_copy(q, s if q <= fwd else -s))

    @pl.when(is_root)
    def _():
        for k in range(CHUNKS):
            u_second(k).start()
            u_copy(u_rows(0, k), s, 0, k).start()
            if bwd:
                u_copy(u_rows(0, k), -s, 1, k).start()

    slots_from(0)

    @pl.when(is_root)
    def _():
        for k in range(CHUNKS):
            u_partner(u_rows(0, k), k).start()
        i_second().start()
        i_source_sends(lambda c: c.start())

    for ia, a in enumerate(ox):
        for ib, b in enumerate(oy):
            src = (lax.rem(x - s * a + 2 * NX, NX) * NY + lax.rem(y - s * b + 2 * NY, NY)) * 8
            dst = (ia * NY + ib) * 8
            inv_rel[dst:dst + 8, :] = inv[pl.ds(pl.multiple_of(src, 8), 8), :]
    parts = [g[:, i * 128:(i + 1) * 128] for i in range(width // 128)]
    while len(parts) < 8:
        parts = parts + parts
    flipped = jnp.concatenate(parts[:8], axis=0).T
    g_col = jnp.concatenate([flipped[:, i:i + 1] for i in range(width // 128)], axis=0)
    depth = work.shape[0]
    place_of = onehot(jnp.broadcast_to(g_col, (width, depth)) == lane_iota((width, depth))).astype(BF16)
    inv_hi, inv_lo = split2(inv_rel[...])
    lpe_hi[...] = dot(inv_hi, place_of).astype(BF16)
    lpe_lo[...] = dot(inv_lo, place_of).astype(BF16)

    hops = max(NX // 2 + NY // 2, fwd + CHUNKS, 4 + fwd)
    for h in range(1, hops + 1):
        for hf in (half_a, half_b):
            hf.inner_round(h)
        for hf in (half_a, half_b):
            hf.outer_round(h)
        for d in (h, -h):
            if d in oz:
                recv(slot_rows(d), zr.at[oz.index(d)])
                slots_from(d)

        k = h - 1 - dist

        @pl.when((k >= 0) & (k < CHUNKS) & jnp.logical_not(is_root))
        def _():
            ref = u_rows(core, k)
            recv(ref, ur.at[k])

            @pl.when(is_second)
            def _():
                u_copy(ref, s, 0, k).start()
                if bwd:
                    u_copy(ref, -s, 1, k).start()

            @pl.when(relays_u)
            def _():
                u_copy(ref, ahead, 0, k).start()

            @pl.when(jnp.logical_not(is_second))
            def _():
                u_partner(ref, k).start()

        if h == 4:
            @pl.when(is_second)
            def _():
                ref = init.at[NZ * SLOTS:2 * NZ * SLOTS]
                recv(ref, imr.at[0])
                i_source_sends(lambda c: c.start())

        m = h - 4 - dist

        @pl.when((m >= 0) & jnp.logical_not(source) & on_fwd & (fwd - m >= df))
        def _():
            q = fwd - m
            recv(i_rows(core, q), ifr.at[q])

            @pl.when(q > df)
            def _():
                i_copy(q, s).start()

        @pl.when((m >= 0) & jnp.logical_not(on_fwd) & (NZ - bwd + m <= df))
        def _():
            q = NZ - bwd + m
            recv(i_rows(core, q), ifr.at[q])

            @pl.when(q < df)
            def _():
                i_copy(q, -s).start()

    for d in oz:
        recv(partner_rows(d), zpr.at[oz.index(d)])

    @pl.when(jnp.logical_not(is_root))
    def _():
        for k in range(CHUNKS):
            recv(u_rows(1 - core, k), upr.at[k])

    w_hi, w_lo = split2(work[...])
    upper = dot(lpe_hi[...], w_hi) + dot(lpe_hi[...], w_lo) + dot(lpe_lo[...], w_hi)
    up_a[...] = upper
    for ia in range(NX):
        for ib in range(NY):
            src, dst = (ia * NY + ib) * 8, (ib * NX + ia) * 8
            up_b[dst:dst + 8, :] = up_a[src:src + 8, :]

    mine_init = init[pl.ds(pl.multiple_of((core * NZ + df) * SLOTS, SLOTS), SLOTS), :]
    parts = split3(mine_init)
    ones = jnp.ones((SLOTS, 128), BF16)
    for n, (buf, up) in enumerate(((buf_a, up_a), (buf_b, up_b))):
        u_hi, u_lo = split2(up[...])
        p_hi, p_lo = split2(buf[...])
        product = dot_t(p_hi, u_hi) + dot_t(p_hi, u_lo) + dot_t(p_lo, u_hi)
        at = slice(n * half_rows, (n + 1) * half_rows)
        place = pick[:, at]
        taken = dot_t(place, ones)
        taken = jnp.concatenate([taken] * (cols // 128), axis=1)
        new = dot_t(place, parts[0]) + dot_t(place, parts[1]) + dot_t(place, parts[2])
        mat[at, :] = jnp.where(taken > 0.5, new, mat[at, :]) - product

    @pl.when(is_root)
    def _():
        for ia, a in enumerate(ox):
            for ib, b in enumerate(oy):
                dst = (lax.rem(x - s * a + 2 * NX, NX) * NY + lax.rem(y - s * b + 2 * NY, NY)) * 8
                src = (ia * NY + ib) * 8
                mat[pl.ds(pl.multiple_of(dst, 8), 8), :] = up_a[src:src + 8, :]

    store = pltpu.make_async_copy(mat, out_any, out_sem.at[0])
    store.start()
    half_a.finish()
    half_b.finish()
    for c in z_sends:
        c.wait_send()

    @pl.when(is_root)
    def _():
        for k in range(CHUNKS):
            u_second(k).wait_send()
            u_copy(u_rows(0, k), s, 0, k).wait_send()
            if bwd:
                u_copy(u_rows(0, k), -s, 1, k).wait_send()
            u_partner(u_rows(0, k), k).wait_send()
        i_second().wait_send()
        i_source_sends(lambda c: c.wait_send())

    @pl.when(is_second)
    def _():
        for k in range(CHUNKS):
            u_copy(u_rows(1, k), s, 0, k).wait_send()
            if bwd:
                u_copy(u_rows(1, k), -s, 1, k).wait_send()
        i_source_sends(lambda c: c.wait_send())

    @pl.when(relays_u)
    def _():
        for k in range(CHUNKS):
            u_copy(u_rows(core, k), ahead, 0, k).wait_send()

    @pl.when(jnp.logical_not(source))
    def _():
        for k in range(CHUNKS):
            u_partner(u_rows(core, k), k).wait_send()

    for q in range(1, NZ):
        if q <= fwd:
            @pl.when(jnp.logical_not(source) & on_fwd & (q > df))
            def _():
                i_copy(q, s).wait_send()
        else:
            @pl.when(jnp.logical_not(on_fwd) & (q < df))
            def _():
                i_copy(q, -s).wait_send()

    store.wait()


def local(matrix, panel_t, inverse_lower, pivot_rows):
    rows, cols = matrix.shape
    width = inverse_lower.shape[0]
    depth = width // 2 + 2 * NZ * SLOTS
    half = panel_t.shape[1] // 2
    anywhere = pl.BlockSpec(memory_space=pl.ANY)
    dma = pltpu.SemaphoreType.DMA
    return pl.pallas_call(
        kernel,
        out_shape=jax.ShapeDtypeStruct((rows, cols), F32),
        in_specs=[anywhere, anywhere, anywhere, pl.BlockSpec(memory_space=pltpu.VMEM)],
        out_specs=anywhere,
        scratch_shapes=[
            pltpu.VMEM((rows, cols), F32),
            pltpu.VMEM((width, width), F32),
            pltpu.VMEM((width, width), F32),
            pltpu.VMEM((width, half), F32),
            pltpu.VMEM((width, half), F32),
            pltpu.VMEM((depth, cols), F32),
            pltpu.VMEM((2 * NZ * SLOTS, cols), F32),
            pltpu.VMEM((width, depth), BF16),
            pltpu.VMEM((width, depth), BF16),
            pltpu.VMEM((width, cols), F32),
            pltpu.VMEM((width, cols), F32),
            dma((4,)), dma((1,)), dma((1,)),
            dma((NY,)), dma((NX, len(groups_of(NY)))),
            dma((NX,)), dma((NY, len(groups_of(NX)))),
            dma((NZ,)), dma((NZ,)), dma((NZ,)), dma((NZ,)),
            dma((3, CHUNKS)), dma((CHUNKS,)), dma((CHUNKS,)), dma((CHUNKS,)),
            dma((1,)), dma((1,)), dma((NZ,)), dma((NZ,)), dma((1,)),
        ],
        compiler_params=pltpu.CompilerParams(
            collective_id=0, has_side_effects=True, vmem_limit_bytes=60 << 20
        ),
    )(matrix, panel_t, inverse_lower, pivot_rows.reshape(1, width))


def solution(mesh):
    in_specs = (P("row", "col"), P("col", "row"), P(), P())
    out_specs = P("row", "col")
    return jax.shard_map(local, mesh=mesh, in_specs=in_specs, out_specs=out_specs, check_vma=False)
```

time: 173 us -> 57.7 us (0.33)
  the two profiles are of different devices: /device:TPU:1 before, /device:TPU:6 now
where the time goes in v1:
time: 57.7 us; the launch traced here: 57.4 us
  Pallas kernels  55.1 us (95%)
  local copies, waits for them, and re-layouts  2.36 us (4%)
    pallas_call x1, Pallas kernels, local(): pl.pallas_call(kernel, out_shape=jax.ShapeDtypeStruct((rows, cols), F32),...  55.1 us
    unnamed x1, local copies, waits for them, and re-layouts  2.36 us

profile of v1, /device:TPU:6, one launch (start us, length us, event | category | flops | bytes accessed | tf_op | source)
XLA Modules:
  0.0 57.4 jit_solution(13677184327194727710)
XLA Ops:
  0.0 55.1 %shard_map.46 = f32[768,384]{1,0:T(8,128)} custom-call(f32[768,384]{1,0:T(8,128)} %mat_any.1, f32[8,768]{1,0:T(8,128)} %pan_any.1, f32[512,512]{1,0:T(8,128)} %inv_any.1, s32[1,512]{1,0:T(1,128)} %bitcast.1), custom_call_target="tpu_custom_call" | custom-call | tf_op jit(solution)/shard_map/pallas_call | solution.py:501
  55.1 2.4 %copy.6 = f32[768,384]{1,0:T(8,128)} copy(f32[768,384]{1,0:T(8,128)} %shard_map.46) | data formatting | bytes 2359296

commit v2 on v1

v2 whole, which is shorter than its diff:
```python
import functools

import jax
import jax.numpy as jnp
from jax import lax
from jax.experimental import pallas as pl
from jax.experimental.pallas import tpu as pltpu
from jax.sharding import PartitionSpec as P

MESH = pl.DeviceIdType.MESH
F32, BF16 = jnp.float32, jnp.bfloat16

NX, NY, NZ = 8, 8, 8
SLOTS = 32


def order_of(n):
    order = [0]
    for d in range(1, n // 2 + 1):
        order.append(d)
        if d <= (n - 1) // 2:
            order.append(-d)
    return order


def groups_of(n):
    order = order_of(n)
    top = n // 2
    groups = [(0, 1, 0)]
    d = 1
    while d <= top:
        last = top if (d + 1 == top and n % 2 == 0) else d
        slots = [i for i, o in enumerate(order) if d <= abs(o) <= last]
        groups.append((slots[0], len(slots), last))
        d = last + 1
    return groups


def split2(v):
    hi = v.astype(BF16)
    return hi, (v - hi.astype(F32)).astype(BF16)


def split3(v):
    hi = v.astype(BF16)
    rest = v - hi.astype(F32)
    mid = rest.astype(BF16)
    return hi, mid, (rest - mid.astype(F32)).astype(BF16)


def dot(a, b):
    return jnp.dot(a, b, preferred_element_type=F32)


def dot_t(a, b):
    return lax.dot_general(a, b, (((0,), (0,)), ((), ())), preferred_element_type=F32)


def select(onehot, v):
    hi, mid, lo = split3(v)
    return dot(onehot, hi) + dot(onehot, mid) + dot(onehot, lo)


def lane_iota(shape):
    return lax.broadcasted_iota(jnp.int32, shape, 1).astype(F32)


def sub_iota(shape):
    return lax.broadcasted_iota(jnp.int32, shape, 0).astype(F32)


def onehot(test):
    return jnp.where(test, 1.0, 0.0)


def kernel(
    mat_any, pan_any, inv_any, piv_ref, out_any,
    mat, inv, inv_rel, buf_a, buf_b, pan_b, work, init, lpe_hi, lpe_lo, w_hi, w_lo, up,
    local_sem, send_a, send_b, a1, a2, b1, b2,
    zs, zr, zps, zpr, us, ur, ups, upr, ims, imr, ifs, ifr, ready, pready, out_sem,
):
    rows, cols = mat.shape
    width = inv.shape[0]
    free = width // 2
    n_row = 2 * NZ
    cls_rows = free // 2
    row, col = lax.axis_index("row"), lax.axis_index("col")
    z, core = row // 2, row % 2
    x, y = col // NY, col % NY
    s = 1 - 2 * core
    first_core = core == 0

    def at_x(d):
        return (row, lax.rem(x + d + 2 * NX, NX) * NY + y)

    def at_y(d):
        return (row, x * NY + lax.rem(y + d + 2 * NY, NY))

    def at_z(t):
        return (t * 2 + core, col)

    partner = (z * 2 + 1 - core, col)

    barrier = pltpu.get_barrier_semaphore()
    for other in (at_x(1), at_x(-1), at_y(1), at_y(-1)):
        pl.semaphore_signal(barrier, inc=1, device_id=other, device_id_type=MESH)
    for t in range(1, NZ):
        @pl.when(z < t)
        def _():
            pl.semaphore_signal(barrier, inc=1, device_id=at_z(t), device_id_type=MESH)

    @pl.when(first_core)
    def _():
        pl.semaphore_signal(barrier, inc=1, device_id=partner, device_id_type=MESH)

    half = pan_any.shape[1] // 2
    loads = [
        pltpu.make_async_copy(mat_any, mat, local_sem.at[0]),
        pltpu.make_async_copy(pan_any.at[:, 0:half], buf_a.at[0:8], local_sem.at[1]),
        pltpu.make_async_copy(pan_any.at[:, half:], buf_b.at[0:8], local_sem.at[2]),
        pltpu.make_async_copy(inv_any, inv, local_sem.at[3]),
    ]
    for load in loads:
        load.start()

    p = piv_ref[...].astype(F32)
    place = lane_iota(p.shape)
    moved = p != place
    owner = jnp.floor((p + 0.5) * (1.0 / rows))
    local_row = p - owner * rows
    cls = jnp.where(moved, owner, 0.0)
    member = onehot(jnp.broadcast_to(cls, (n_row, width)) == sub_iota((n_row, width)))
    before = onehot(sub_iota((width, width)) < lane_iota((width, width))).astype(BF16)
    counts = dot(member.astype(BF16), before)
    rank = jnp.sum(member * counts, axis=0, keepdims=True)
    g = jnp.where(moved, free + SLOTS * owner + rank, rank)

    mine = onehot(
        jnp.broadcast_to(g, (SLOTS, width))
        == sub_iota((SLOTS, width)) + (free + SLOTS * row).astype(F32)
    )
    spot = jnp.sum(mine * local_row, axis=1, keepdims=True)
    used = jnp.sum(mine, axis=1, keepdims=True)
    spot = jnp.where(used > 0.0, spot, -1.0)
    pick = onehot(jnp.broadcast_to(spot, (SLOTS, rows)) == lane_iota((SLOTS, rows))).astype(BF16)

    def slots(t, c):
        return work.at[pl.ds(pl.multiple_of(free + SLOTS * (2 * t + c), SLOTS), SLOTS)]

    loads[0].wait()
    slots(z, core)[...] = select(pick, mat[...])

    is_root = row == 0
    source = z == 0

    @pl.when(is_root)
    def _():
        head = mat[0:width, :]
        unmoved = onehot(jnp.broadcast_to(g, (free, width)) == sub_iota((free, width))).astype(BF16)
        work[0:free, :] = select(unmoved, head)
        owner_z = jnp.floor((owner + 0.5) * 0.5)
        owner_c = owner - 2.0 * owner_z
        goal = jnp.where(moved, (owner_c * NZ + owner_z) * SLOTS + rank, -1.0)
        total = n_row * SLOTS
        send_to = onehot(jnp.broadcast_to(goal, (total, width)) == sub_iota((total, width))).astype(BF16)
        init[...] = select(send_to, head)

    for load in loads[1:]:
        load.wait()
    pl.semaphore_wait(barrier, 4 + z + core)

    def copy(src, dst, ss, rs, to):
        return pltpu.make_async_remote_copy(
            src_ref=src, dst_ref=dst, send_sem=ss, recv_sem=rs, device_id=to, device_id_type=MESH
        )

    def send(src, dst, ss, rs, to):
        copy(src, dst, ss, rs, to).start()

    def recv(ref, sem):
        pltpu.make_async_copy(ref, ref, sem).wait()

    def own_slots(t):
        ref = slots(z, core)
        return copy(ref, ref, zs.at[t], zr.at[z], at_z(t))

    def pass_slots(t):
        ref = slots(t, core)
        return copy(ref, ref, zps.at[t], zpr.at[t], partner)

    def u_rows(c):
        return work.at[pl.ds(pl.multiple_of(c * cls_rows, cls_rows), cls_rows)]

    def u_copy(t):
        ref = u_rows(core)
        return copy(ref, ref, us.at[t], ur.at[0], at_z(t))

    def u_second():
        ref = u_rows(1)
        return copy(ref, ref, us.at[0], ur.at[0], partner)

    def u_pass():
        ref = u_rows(core)
        return copy(ref, ref, ups.at[0], upr.at[0], partner)

    def i_rows(t):
        return init.at[pl.ds(pl.multiple_of((core * NZ + t) * SLOTS, SLOTS), SLOTS)]

    def i_copy(t):
        return copy(i_rows(t), i_rows(t), ifs.at[t], ifr.at[0], at_z(t))

    i_half = init.at[NZ * SLOTS:2 * NZ * SLOTS]

    def i_second():
        return copy(i_half, i_half, ims.at[0], imr.at[0], partner)

    for t in range(NZ - 1):
        @pl.when(t < z)
        def _():
            pl.semaphore_signal(ready.at[z], inc=1, device_id=at_z(t), device_id_type=MESH)
            own_slots(t).start()

    @pl.when(jnp.logical_not(first_core))
    def _():
        pl.semaphore_signal(pready, inc=1, device_id=partner, device_id_type=MESH)
        pass_slots(z).start()

    ox, oy = order_of(NX), order_of(NY)

    class Half:
        def __init__(self, buf, first, second, n_in, n_out, at_in, at_out, send_sem):
            self.buf, self.first, self.second = buf, first, second
            self.n_in, self.n_out = n_in, n_out
            self.at_in, self.at_out = at_in, at_out
            self.o_in, self.o_out = order_of(n_in), order_of(n_out)
            self.groups = groups_of(n_in)
            self.send_sem = send_sem

        def span(self, o, i0, n):
            base = (self.o_out.index(o) * self.n_in + i0) * 8
            return self.buf.at[base:base + n * 8]

        def next_ones(self, d, n):
            out = []
            if 0 <= d < n // 2:
                out.append(d + 1)
            if 0 >= d > -((n - 1) // 2):
                out.append(d - 1)
            return out

        def inner_from(self, d):
            i = self.o_in.index(d)
            for t in self.next_ones(d, self.n_in):
                j = self.o_in.index(t)
                step = 1 if t > 0 else -1
                send(self.span(0, i, 1), self.span(0, j, 1), self.send_sem, self.first.at[j], self.at_in(step * s))

        def outer_from(self, o, k):
            i0, n, _ = self.groups[k]
            for t in self.next_ones(o, self.n_out):
                step = 1 if t > 0 else -1
                send(
                    self.span(o, i0, n), self.span(t, i0, n), self.send_sem,
                    self.second.at[self.o_out.index(t), k], self.at_out(step * s),
                )

        def inner_round(self, h):
            for d in (h, -h):
                if d in self.o_in:
                    i = self.o_in.index(d)
                    recv(self.span(0, i, 1), self.first.at[i])
                    self.inner_from(d)
            for k, (_, _, hops) in enumerate(self.groups):
                if hops == h:
                    self.outer_from(0, k)

        def outer_round(self, h):
            for k, (i0, n, hops) in enumerate(self.groups):
                for o in (h - hops, hops - h):
                    if o != 0 and h > hops and o in self.o_out:
                        recv(self.span(o, i0, n), self.second.at[self.o_out.index(o), k])
                        self.outer_from(o, k)

        def finish(self):
            ref = self.buf.at[0:(self.n_in * self.n_out - 1) * 8]
            pltpu.make_async_copy(ref, ref, self.send_sem).wait()

    half_a = Half(buf_a, a1, a2, NY, NX, at_y, at_x, send_a.at[0])
    half_b = Half(buf_b, b1, b2, NX, NY, at_x, at_y, send_b.at[0])
    for h in (half_a, half_b):
        h.outer_from(0, 0)
        h.inner_from(0)

    for ia, a in enumerate(ox):
        for ib, b in enumerate(oy):
            src = (lax.rem(x - s * a + 2 * NX, NX) * NY + lax.rem(y - s * b + 2 * NY, NY)) * 8
            dst = (ia * NY + ib) * 8
            inv_rel[dst:dst + 8, :] = inv[pl.ds(pl.multiple_of(src, 8), 8), :]
    parts = [g[:, i * 128:(i + 1) * 128] for i in range(width // 128)]
    while len(parts) < 8:
        parts = parts + parts
    flipped = jnp.concatenate(parts[:8], axis=0).T
    g_col = jnp.concatenate([flipped[:, i:i + 1] for i in range(width // 128)], axis=0)
    depth = work.shape[0]
    place_of = onehot(jnp.broadcast_to(g_col, (width, depth)) == lane_iota((width, depth))).astype(BF16)
    inv_hi, inv_lo = split2(inv_rel[...])
    lpe_hi[...] = dot(inv_hi, place_of).astype(BF16)
    lpe_lo[...] = dot(inv_lo, place_of).astype(BF16)

    for h in range(1, NX // 2 + NY // 2 + 1):
        for hf in (half_a, half_b):
            hf.inner_round(h)
        for hf in (half_a, half_b):
            hf.outer_round(h)

    @pl.when(first_core)
    def _():
        pl.semaphore_wait(pready, 1)

        @pl.when(source)
        def _():
            u_second().start()
            u_pass().start()
            i_second().start()

        pass_slots(z).start()

    @pl.when(jnp.logical_not(is_root))
    def _():
        recv(u_rows(core), ur.at[0])

        @pl.when(jnp.logical_not(source))
        def _():
            u_pass().start()

        @pl.when(source)
        def _():
            recv(i_half, imr.at[0])

    def along_z(lo, hi):
        for t in range(lo, hi):
            @pl.when(z < t)
            def _():
                pl.semaphore_wait(ready.at[t], 1)

                @pl.when(source)
                def _():
                    u_copy(t).start()
                    i_copy(t).start()

                own_slots(t).start()

            @pl.when(z != t)
            def _():
                recv(slots(t, core), zr.at[t])
                pass_slots(t).start()

    def other_core(lo, hi):
        for t in range(lo, hi):
            recv(slots(t, 1 - core), zpr.at[t])

    for ib in range(NY):
        for ia in range(NX):
            src, dst = (ib * NX + ia) * 8, (ia * NY + ib) * 8
            pan_b[dst:dst + 8, :] = buf_b[src:src + 8, :]
    for n, buf in enumerate((buf_a, pan_b)):
        at = slice(n * half, (n + 1) * half)
        p_hi, p_lo = split2(buf[...])
        w = dot_t(p_hi, lpe_hi[...]) + dot_t(p_hi, lpe_lo[...]) + dot_t(p_lo, lpe_hi[...])
        w_hi[at, :], w_lo[at, :] = split2(w)

    cut = free + n_row * SLOTS // 2
    along_z(0, NZ // 2)

    @pl.when(jnp.logical_not(source))
    def _():
        recv(i_rows(z), ifr.at[0])

    @pl.when(jnp.logical_not(is_root))
    def _():
        recv(u_rows(1 - core), upr.at[0])

    other_core(0, NZ // 2)

    def product(l_hi, l_lo, v):
        v_hi, v_lo = split2(v)
        return dot(l_hi, v_hi) + dot(l_hi, v_lo) + dot(l_lo, v_hi)

    parts = split3(i_rows(z)[...])
    ones = jnp.ones((SLOTS, 128), BF16)
    v_hi, v_lo = split2(work[0:cut, :])
    for n in range(2):
        at = slice(n * half, (n + 1) * half)
        place = pick[:, at]
        taken = dot_t(place, ones)
        taken = jnp.concatenate([taken] * (cols // 128), axis=1)
        new = dot_t(place, parts[0]) + dot_t(place, parts[1]) + dot_t(place, parts[2])
        early = dot(w_hi[at, 0:cut], v_hi) + dot(w_hi[at, 0:cut], v_lo) + dot(w_lo[at, 0:cut], v_hi)
        mat[at, :] = jnp.where(taken > 0.5, new, mat[at, :]) - early

    @pl.when(is_root)
    def _():
        up[...] = product(lpe_hi[:, 0:cut], lpe_lo[:, 0:cut], work[0:cut, :])

    along_z(NZ // 2, NZ)
    other_core(NZ // 2, NZ)

    v_hi, v_lo = split2(work[cut:, :])
    for n in range(2):
        at = slice(n * half, (n + 1) * half)
        late = dot(w_hi[at, cut:], v_hi) + dot(w_hi[at, cut:], v_lo) + dot(w_lo[at, cut:], v_hi)
        mat[at, :] = mat[at, :] - late

    @pl.when(is_root)
    def _():
        up[...] += product(lpe_hi[:, cut:], lpe_lo[:, cut:], work[cut:, :])
        for ia, a in enumerate(ox):
            for ib, b in enumerate(oy):
                dst = (lax.rem(x - s * a + 2 * NX, NX) * NY + lax.rem(y - s * b + 2 * NY, NY)) * 8
                src = (ia * NY + ib) * 8
                mat[pl.ds(pl.multiple_of(dst, 8), 8), :] = up[src:src + 8, :]

    store = pltpu.make_async_copy(mat, out_any, out_sem.at[0])
    store.start()
    half_a.finish()
    half_b.finish()
    for t in range(NZ):
        @pl.when(z != t)
        def _():
            own_slots(t).wait_send()

            @pl.when(source)
            def _():
                u_copy(t).wait_send()
                i_copy(t).wait_send()

        pass_slots(t).wait_send()

    @pl.when(is_root)
    def _():
        u_second().wait_send()
        i_second().wait_send()

    @pl.when(jnp.logical_or(is_root, jnp.logical_not(source)))
    def _():
        u_pass().wait_send()

    store.wait()


def local(matrix, panel_t, inverse_lower, pivot_rows):
    rows, cols = matrix.shape
    width = inverse_lower.shape[0]
    depth = width // 2 + 2 * NZ * SLOTS
    half = panel_t.shape[1] // 2
    anywhere = pl.BlockSpec(memory_space=pl.ANY)
    dma, regular = pltpu.SemaphoreType.DMA, pltpu.SemaphoreType.REGULAR
    return pl.pallas_call(
        kernel,
        out_shape=jax.ShapeDtypeStruct((rows, cols), F32),
        in_specs=[anywhere, anywhere, anywhere, pl.BlockSpec(memory_space=pltpu.VMEM)],
        out_specs=anywhere,
        scratch_shapes=[
            pltpu.VMEM((rows, cols), F32),
            pltpu.VMEM((width, width), F32),
            pltpu.VMEM((width, width), F32),
            pltpu.VMEM((width, half), F32),
            pltpu.VMEM((width, half), F32),
            pltpu.VMEM((width, half), F32),
            pltpu.VMEM((depth, cols), F32),
            pltpu.VMEM((2 * NZ * SLOTS, cols), F32),
            pltpu.VMEM((width, depth), BF16),
            pltpu.VMEM((width, depth), BF16),
            pltpu.VMEM((rows, depth), BF16),
            pltpu.VMEM((rows, depth), BF16),
            pltpu.VMEM((width, cols), F32),
            dma((4,)), dma((1,)), dma((1,)),
            dma((NY,)), dma((NX, len(groups_of(NY)))),
            dma((NX,)), dma((NY, len(groups_of(NX)))),
            dma((NZ,)), dma((NZ,)), dma((NZ,)), dma((NZ,)),
            dma((NZ,)), dma((1,)), dma((1,)), dma((1,)),
            dma((1,)), dma((1,)), dma((NZ,)), dma((1,)),
            regular((NZ,)), regular, dma((1,)),
        ],
        compiler_params=pltpu.CompilerParams(
            collective_id=0, has_side_effects=True, vmem_limit_bytes=60 << 20
        ),
    )(matrix, panel_t, inverse_lower, pivot_rows.reshape(1, width))


def solution(mesh):
    in_specs = (P("row", "col"), P("col", "row"), P(), P())
    out_specs = P("row", "col")
    return jax.shard_map(local, mesh=mesh, in_specs=in_specs, out_specs=out_specs, check_vma=False)
```

time: 57.7 us -> 93.9 us (1.63)
  the two profiles are of different devices: /device:TPU:6 before, /device:TPU:897 now
where the time goes in v2:
time: 93.9 us; the launch traced here: 93.7 us
  Pallas kernels  91.3 us (97%)
  local copies, waits for them, and re-layouts  2.36 us (3%)
    pallas_call x1, Pallas kernels, local(): pl.pallas_call(kernel, out_shape=jax.ShapeDtypeStruct((rows, cols), F32),...  91.3 us
    unnamed x1, local copies, waits for them, and re-layouts  2.36 us

profile of v2, /device:TPU:897, one launch (start us, length us, event | category | flops | bytes accessed | tf_op | source)
XLA Modules:
  0.0 93.7 jit_solution(6641078347421340555)
XLA Ops:
  0.0 91.3 %shard_map.46 = f32[768,384]{1,0:T(8,128)} custom-call(f32[768,384]{1,0:T(8,128)} %mat_any.1, f32[8,768]{1,0:T(8,128)} %pan_any.1, f32[512,512]{1,0:T(8,128)} %inv_any.1, s32[1,512]{1,0:T(1,128)} %bitcast.1), custom_call_target="tpu_custom_call" | custom-call | tf_op jit(solution)/shard_map/pallas_call | solution.py:458
  91.3 2.4 %copy.6 = f32[768,384]{1,0:T(8,128)} copy(f32[768,384]{1,0:T(8,128)} %shard_map.46) | data formatting | bytes 2359296

commit v3 on v2

v3 whole, which is shorter than its diff:
```python
import functools

import jax
import jax.numpy as jnp
from jax import lax
from jax.experimental import pallas as pl
from jax.experimental.pallas import tpu as pltpu
from jax.sharding import PartitionSpec as P

MESH = pl.DeviceIdType.MESH
UPPER = 99.0
HOP = 3.0
F32, BF16 = jnp.float32, jnp.bfloat16

NX, NY, NZ = 8, 8, 8
SLOTS = 32


def order_of(n):
    order = [0]
    for d in range(1, n // 2 + 1):
        order.append(d)
        if d <= (n - 1) // 2:
            order.append(-d)
    return order


def groups_of(n):
    order = order_of(n)
    top = n // 2
    groups = [(0, 1, 0)]
    d = 1
    while d <= top:
        last = top if (d + 1 == top and n % 2 == 0) else d
        slots = [i for i, o in enumerate(order) if d <= abs(o) <= last]
        groups.append((slots[0], len(slots), last))
        d = last + 1
    return groups


def split2(v):
    hi = v.astype(BF16)
    return hi, (v - hi.astype(F32)).astype(BF16)


def dot(a, b):
    return jnp.dot(a, b, preferred_element_type=F32)


def dot_t(a, b):
    return lax.dot_general(a, b, (((0,), (0,)), ((), ())), preferred_element_type=F32)


def select(onehot, v):
    hi, lo = split2(v)
    return dot(onehot, hi) + dot(onehot, lo)


def lane_iota(shape):
    return lax.broadcasted_iota(jnp.int32, shape, 1).astype(F32)


def sub_iota(shape):
    return lax.broadcasted_iota(jnp.int32, shape, 0).astype(F32)


def onehot(test):
    return jnp.where(test, 1.0, 0.0)


def kernel(
    mat_any, pan_any, inv_any, piv_ref, mat,
    inv, inv_rel, buf_a, buf_b, work, init, lpe_hi, lpe_lo, up, up_b,
    local_sem, send_a, send_b, a1, a2, b1, b2,
    zs, zr, zps, zpr, us, ur, ups, upr, ims, imr, ifs, ifr, ready, pready,
):
    rows, cols = mat.shape
    width = inv.shape[0]
    free = width // 2
    n_row = 2 * NZ
    row, col = lax.axis_index("row"), lax.axis_index("col")
    z, core = row // 2, row % 2
    x, y = col // NY, col % NY
    s = 1 - 2 * core
    first_core = core == 0

    def at_x(d):
        return (row, lax.rem(x + d + 2 * NX, NX) * NY + y)

    def at_y(d):
        return (row, x * NY + lax.rem(y + d + 2 * NY, NY))

    def at_z(t):
        return (t * 2 + core, col)

    partner = (z * 2 + 1 - core, col)

    barrier = pltpu.get_barrier_semaphore()
    for other in [at_x(d) for d in range(1, NX)] + [at_y(d) for d in range(1, NY)]:
        pl.semaphore_signal(barrier, inc=1, device_id=other, device_id_type=MESH)
    for t in range(1, NZ):
        @pl.when(z < t)
        def _():
            pl.semaphore_signal(barrier, inc=1, device_id=at_z(t), device_id_type=MESH)

    @pl.when(first_core)
    def _():
        pl.semaphore_signal(barrier, inc=1, device_id=partner, device_id_type=MESH)

    half = pan_any.shape[1] // 2
    loads = [
        pltpu.make_async_copy(pan_any.at[:, 0:half], buf_a.at[0:8], local_sem.at[0]),
        pltpu.make_async_copy(pan_any.at[:, half:], buf_b.at[0:8], local_sem.at[1]),
        pltpu.make_async_copy(mat_any, mat, local_sem.at[2]),
        pltpu.make_async_copy(inv_any, inv, local_sem.at[3]),
    ]
    for load in loads:
        load.start()

    for load in loads[:2]:
        load.wait()
    pl.semaphore_wait(barrier, NX + NY - 2 + z + core)

    def copy(src, dst, ss, rs, to):
        return pltpu.make_async_remote_copy(
            src_ref=src, dst_ref=dst, send_sem=ss, recv_sem=rs, device_id=to, device_id_type=MESH
        )

    def send(src, dst, ss, rs, to):
        copy(src, dst, ss, rs, to).start()

    def recv(ref, sem):
        pltpu.make_async_copy(ref, ref, sem).wait()

    def slots(t, c):
        return work.at[pl.ds(pl.multiple_of(free + SLOTS * (2 * t + c), SLOTS), SLOTS)]

    is_root = row == 0
    source = z == 0

    def own_slots(t):
        ref = slots(z, core)
        return copy(ref, ref, zs.at[t], zr.at[z], at_z(t))

    def pass_slots(t):
        ref = slots(t, core)
        return copy(ref, ref, zps.at[t], zpr.at[t], partner)

    u_rows = work.at[0:free]

    def u_copy(t):
        return copy(u_rows, u_rows, us.at[t], ur.at[0], at_z(t))

    def u_pass():
        return copy(u_rows, u_rows, ups.at[0], upr.at[0], partner)

    def i_pair(t):
        return init.at[pl.ds(pl.multiple_of(2 * t * SLOTS, 2 * SLOTS), 2 * SLOTS)]

    def i_copy(t):
        return copy(i_pair(t), i_pair(t), ifs.at[t], ifr.at[0], at_z(t))

    def i_rows(c):
        return init.at[pl.ds(pl.multiple_of((2 * z + c) * SLOTS, SLOTS), SLOTS)]

    def i_pass():
        return copy(i_rows(1), i_rows(1), ims.at[0], imr.at[0], partner)

    for t in range(NZ - 1):
        @pl.when(t < z)
        def _():
            pl.semaphore_signal(ready.at[z], inc=1, device_id=at_z(t), device_id_type=MESH)

    @pl.when(jnp.logical_not(first_core))
    def _():
        pl.semaphore_signal(pready, inc=1, device_id=partner, device_id_type=MESH)

    def root_serve(t):
        pl.semaphore_wait(ready.at[t], 1)
        u_copy(t).start()
        i_copy(t).start()
        own_slots(t).start()

    ox, oy = order_of(NX), order_of(NY)

    class Half:
        def __init__(self, buf, first, second, n_in, n_out, at_in, at_out, send_sem):
            self.buf, self.first, self.second = buf, first, second
            self.n_in, self.n_out = n_in, n_out
            self.at_in, self.at_out = at_in, at_out
            self.o_in, self.o_out = order_of(n_in), order_of(n_out)
            self.groups = groups_of(n_in)
            self.send_sem = send_sem

        def span(self, o, i0, n):
            base = (self.o_out.index(o) * self.n_in + i0) * 8
            return self.buf.at[base:base + n * 8]

        def next_ones(self, d, n):
            out = []
            if 0 <= d < n // 2:
                out.append(d + 1)
            if 0 >= d > -((n - 1) // 2):
                out.append(d - 1)
            return out

        def inner_sends(self):
            own = self.span(0, 0, 1)
            for j, d in enumerate(self.o_in):
                if j:
                    send(own, self.span(0, j, 1), self.send_sem, self.first.at[j], self.at_in(d * s))

        def outer_from(self, o, k):
            i0, n, _ = self.groups[k]
            for t in self.next_ones(o, self.n_out):
                step = 1 if t > 0 else -1
                send(
                    self.span(o, i0, n), self.span(t, i0, n), self.send_sem,
                    self.second.at[self.o_out.index(t), k], self.at_out(step * s),
                )

        def arrive(self, o, k):
            i0, n, _ = self.groups[k]
            if o:
                recv(self.span(o, i0, n), self.second.at[self.o_out.index(o), k])
            else:
                for i in range(i0, i0 + n):
                    recv(self.span(0, i, 1), self.first.at[i])
            self.outer_from(o, k)

        def events(self):
            out = []
            for k, (_, _, hops) in enumerate(self.groups):
                for o in self.o_out:
                    if k or o:
                        start = 0.9 + 0.75 * hops if k else 0.0
                        out.append((start + HOP * abs(o), self, o, k))
            return out

        def finish(self):
            ref = self.buf.at[0:(self.n_in * self.n_out - 1) * 8]
            pltpu.make_async_copy(ref, ref, self.send_sem).wait()

    half_a = Half(buf_a, a1, a2, NY, NX, at_y, at_x, send_a.at[0])
    half_b = Half(buf_b, b1, b2, NX, NY, at_x, at_y, send_b.at[0])
    for h in (half_a, half_b):
        h.outer_from(0, 0)
        h.inner_sends()

    p = piv_ref[...].astype(F32)
    place = lane_iota(p.shape)
    moved = p != place
    owner = jnp.floor((p + 0.5) * (1.0 / rows))
    local_row = p - owner * rows
    cls = jnp.where(moved, owner, 0.0)
    member = onehot(jnp.broadcast_to(cls, (n_row, width)) == sub_iota((n_row, width)))
    before = onehot(sub_iota((width, width)) < lane_iota((width, width))).astype(BF16)
    counts = dot(member.astype(BF16), before)
    rank = jnp.sum(member * counts, axis=0, keepdims=True)
    g = jnp.where(moved, free + SLOTS * owner + rank, rank)

    mine = onehot(
        jnp.broadcast_to(g, (SLOTS, width))
        == sub_iota((SLOTS, width)) + (free + SLOTS * row).astype(F32)
    )
    spot = jnp.sum(mine * local_row, axis=1, keepdims=True)
    used = jnp.sum(mine, axis=1, keepdims=True)
    spot = jnp.where(used > 0.0, spot, -1.0)
    pick = onehot(jnp.broadcast_to(spot, (SLOTS, rows)) == lane_iota((SLOTS, rows))).astype(BF16)

    loads[2].wait()
    slots(z, core)[...] = select(pick, mat[...])

    @pl.when(is_root)
    def _():
        head = mat[0:width, :]
        unmoved = onehot(jnp.broadcast_to(g, (free, width)) == sub_iota((free, width))).astype(BF16)
        work[0:free, :] = select(unmoved, head)
        goal = jnp.where(moved, owner * SLOTS + rank, -1.0)
        total = n_row * SLOTS
        send_to = onehot(jnp.broadcast_to(goal, (total, width)) == sub_iota((total, width))).astype(BF16)
        init[...] = select(send_to, head)

    for t in range(NZ - 1):
        @pl.when(t < z)
        def _():
            own_slots(t).start()

    @pl.when(jnp.logical_not(first_core))
    def _():
        pass_slots(z).start()

    @pl.when(first_core)
    def _():
        pl.semaphore_wait(pready, 1)
        pass_slots(z).start()

    @pl.when(is_root)
    def _():
        u_pass().start()
        i_pass().start()
        for t in range(1, NZ // 2 + 1):
            root_serve(t)


    def permute_inverse():
        loads[3].wait()
        for ia, a in enumerate(ox):
            for ib, b in enumerate(oy):
                src = (lax.rem(x - s * a + 2 * NX, NX) * NY + lax.rem(y - s * b + 2 * NY, NY)) * 8
                dst = (ia * NY + ib) * 8
                inv_rel[dst:dst + 8, :] = inv[pl.ds(pl.multiple_of(src, 8), 8), :]
        parts = [g[:, i * 128:(i + 1) * 128] for i in range(width // 128)]
        while len(parts) < 8:
            parts = parts + parts
        flipped = jnp.concatenate(parts[:8], axis=0).T
        g_col = jnp.concatenate([flipped[:, i:i + 1] for i in range(width // 128)], axis=0)
        depth = work.shape[0]
        place_of = onehot(jnp.broadcast_to(g_col, (width, depth)) == lane_iota((width, depth))).astype(BF16)
        inv_hi, inv_lo = split2(inv_rel[...])
        lpe_hi[...] = dot(inv_hi, place_of).astype(BF16)
        lpe_lo[...] = dot(inv_lo, place_of).astype(BF16)

    def serve(q):
        t = z + q

        @pl.when((t < NZ) & jnp.logical_not(is_root))
        def _():
            pl.semaphore_wait(ready.at[t], 1)
            own_slots(t).start()

    def finish_upper():
        far_first = first_core & jnp.logical_not(source)

        @pl.when(far_first)
        def _():
            recv(u_rows, ur.at[0])
            u_pass().start()
            recv(i_pair(z), ifr.at[0])
            i_pass().start()

        def along_z(lo, hi):
            for t in range(lo, hi):
                @pl.when(z != t)
                def _():
                    recv(slots(t, core), zr.at[t])
                    pass_slots(t).start()

        def other_core(lo, hi):
            for t in range(lo, hi):
                recv(slots(t, 1 - core), zpr.at[t])

        along_z(0, NZ)

        @pl.when(jnp.logical_not(first_core))
        def _():
            recv(u_rows, upr.at[0])
            recv(i_rows(1), imr.at[0])

        other_core(0, NZ)

        v_hi, v_lo = split2(work[...])
        up[...] = dot(lpe_hi[...], v_hi) + dot(lpe_hi[...], v_lo) + dot(lpe_lo[...], v_hi)
        for ia in range(NX):
            for ib in range(NY):
                src, dst = (ia * NY + ib) * 8, (ib * NX + ia) * 8
                up_b[dst:dst + 8, :] = up[src:src + 8, :]

    leaves = []
    todo = [e for e in half_a.events() + half_b.events()]
    todo += [(1.5 + 1.05 * q, serve, q, 0) for q in range(1, NZ)]
    todo += [(1.5 * (t - NZ // 2 + 1), root_serve, t, 0) for t in range(NZ // 2 + 1, NZ)]
    todo.append((UPPER, finish_upper, 0, 0))
    todo.append((6.0, permute_inverse, 0, 0))
    for e in sorted(todo, key=lambda e: e[0]):
        _, what, o, k = e
        if what is serve:
            serve(o)
        elif what is root_serve:
            pl.when(is_root)(functools.partial(root_serve, o))
        elif what in (permute_inverse, finish_upper):
            what()
        elif o and not what.next_ones(o, what.n_out):
            leaves.append((what, o, k))
        else:
            what.arrive(o, k)

    parts = split2(i_rows(core)[...])
    ones = jnp.ones((SLOTS, 128), BF16)
    halves = []
    for n, (hf, u) in enumerate(((half_a, up), (half_b, up_b))):
        inner = sum(1 for o in hf.o_out if hf.next_ones(o, hf.n_out)) * hf.n_in * 8
        halves.append((slice(n * half, (n + 1) * half), hf, u, inner))

    def part(hf, u, k):
        p_hi, p_lo = split2(hf.buf[k, :])
        u_hi, u_lo = split2(u[k, :])
        return dot_t(p_hi, u_hi) + dot_t(p_hi, u_lo) + dot_t(p_lo, u_hi)

    for at, hf, u, inner in halves:
        place = pick[:, at]
        taken = dot_t(place, ones)
        taken = jnp.concatenate([taken] * (cols // 128), axis=1)
        new = dot_t(place, parts[0]) + dot_t(place, parts[1])
        mat[at, :] = jnp.where(taken > 0.5, new, mat[at, :]) - part(hf, u, slice(0, inner))

    for hf, o, k in leaves:
        hf.arrive(o, k)

    for at, hf, u, inner in halves:
        mat[at, :] = mat[at, :] - part(hf, u, slice(inner, width))

    @pl.when(is_root)
    def _():
        for ia, a in enumerate(ox):
            for ib, b in enumerate(oy):
                dst = (lax.rem(x - s * a + 2 * NX, NX) * NY + lax.rem(y - s * b + 2 * NY, NY)) * 8
                src = (ia * NY + ib) * 8
                mat[pl.ds(pl.multiple_of(dst, 8), 8), :] = up[src:src + 8, :]

    half_a.finish()
    half_b.finish()
    for t in range(NZ):
        @pl.when(z != t)
        def _():
            own_slots(t).wait_send()

        pass_slots(t).wait_send()

    @pl.when(is_root)
    def _():
        for t in range(1, NZ):
            u_copy(t).wait_send()
            i_copy(t).wait_send()

    @pl.when(first_core)
    def _():
        u_pass().wait_send()
        i_pass().wait_send()


def local(matrix, panel_t, inverse_lower, pivot_rows):
    rows, cols = matrix.shape
    width = inverse_lower.shape[0]
    depth = width // 2 + 2 * NZ * SLOTS
    half = panel_t.shape[1] // 2
    hbm, vmem = pl.BlockSpec(memory_space=pltpu.HBM), pl.BlockSpec(memory_space=pltpu.VMEM)
    dma, regular = pltpu.SemaphoreType.DMA, pltpu.SemaphoreType.REGULAR
    held = [pltpu.with_memory_space_constraint(v, pltpu.HBM) for v in (matrix, panel_t, inverse_lower)]
    return pl.pallas_call(
        kernel,
        out_shape=jax.ShapeDtypeStruct((rows, cols), F32),
        in_specs=[hbm, hbm, hbm, vmem],
        out_specs=vmem,
        scratch_shapes=[
            pltpu.VMEM((width, width), F32),
            pltpu.VMEM((width, width), F32),
            pltpu.VMEM((width, half), F32),
            pltpu.VMEM((width, half), F32),
            pltpu.VMEM((depth, cols), F32),
            pltpu.VMEM((2 * NZ * SLOTS, cols), F32),
            pltpu.VMEM((width, depth), BF16),
            pltpu.VMEM((width, depth), BF16),
            pltpu.VMEM((width, cols), F32),
            pltpu.VMEM((width, cols), F32),
            dma((4,)), dma((1,)), dma((1,)),
            dma((NY,)), dma((NX, len(groups_of(NY)))),
            dma((NX,)), dma((NY, len(groups_of(NX)))),
            dma((NZ,)), dma((NZ,)), dma((NZ,)), dma((NZ,)),
            dma((NZ,)), dma((1,)), dma((1,)), dma((1,)),
            dma((1,)), dma((1,)), dma((NZ,)), dma((1,)),
            regular((NZ,)), regular,
        ],
        compiler_params=pltpu.CompilerParams(
            collective_id=0, has_side_effects=True, vmem_limit_bytes=20 << 20
        ),
    )(*held, pivot_rows.reshape(1, width))


def solution(mesh):
    in_specs = (P("row", "col"), P("col", "row"), P(), P())
    out_specs = P("row", "col")
    return jax.shard_map(local, mesh=mesh, in_specs=in_specs, out_specs=out_specs, check_vma=False)
```

time: 93.9 us -> 49.2 us (0.52)
  the two profiles are of different devices: /device:TPU:897 before, /device:TPU:4 now
where the time goes in v3:
time: 49.2 us; the launch traced here: 49 us
  Pallas kernels  47.3 us (96%)
  local copies, waits for them, and re-layouts  1.7 us (3%)
    pallas_call x1, Pallas kernels, local(): pl.pallas_call(kernel, out_shape=jax.ShapeDtypeStruct((rows, cols), F32),...  47.3 us
    unnamed x3, local copies, waits for them, and re-layouts  1.7 us

profile of v3, /device:TPU:4, one launch (start us, length us, event | category | flops | bytes accessed | tf_op | source)
XLA Modules:
  0.0 49.0 jit_solution(14550725089392377107)
XLA Ops:
  0.0 0.0 copy-start
  0.0 0.7 %copy-done = s32[512]{0:T(512)S(1)} copy-done((s32[512]{0:T(512)S(1)}, s32[512]{0:T(512)}, u32[]{:S(2)}) %copy-start) | copy-done | bytes 2072
  0.7 47.3 %shard_map.46 = f32[768,384]{1,0:T(8,128)S(1)} custom-call(f32[768,384]{1,0:T(8,128)} %mat_any.1, f32[8,768]{1,0:T(8,128)} %pan_any.1, f32[512,512]{1,0:T(8,128)} %inv_any.1, s32[1,512]{1,0:T(1,128)S(1)} %bitcast.1), custom_call_target="tpu_custom_call" | custom-call | tf_op jit(solution)/shard_map/pallas_call | solution.py:450
  48.0 1.0 %copy.6 = f32[768,384]{1,0:T(8,128)} copy(f32[768,384]{1,0:T(8,128)S(1)} %shard_map.46) | data formatting | bytes 2359296
Async XLA Ops:
  0.0 0.7 %copy-start = (s32[512]{0:T(512)S(1)}, s32[512]{0:T(512)}, u32[]{:S(2)}) copy-start(s32[512]{0:T(512)} %param.7) | copy-start | bytes 6148

commit v4 on v3

--- a/solution.py
+++ b/solution.py
@@ -371,7 +371,7 @@
     todo += [(1.5 + 1.05 * q, serve, q, 0) for q in range(1, NZ)]
     todo += [(1.5 * (t - NZ // 2 + 1), root_serve, t, 0) for t in range(NZ // 2 + 1, NZ)]
     todo.append((UPPER, finish_upper, 0, 0))
-    todo.append((6.0, permute_inverse, 0, 0))
+    todo.append((0.0, permute_inverse, 0, 0))
     for e in sorted(todo, key=lambda e: e[0]):
         _, what, o, k = e
         if what is serve:

time: 49.2 us -> 49.2 us (level)
  no operation moved by 1% of the time
where the time goes in v4:
time: 49.2 us; the launch traced here: 49 us
  Pallas kernels  47.3 us (96%)
  local copies, waits for them, and re-layouts  1.7 us (3%)
    pallas_call x1, Pallas kernels, local(): pl.pallas_call(kernel, out_shape=jax.ShapeDtypeStruct((rows, cols), F32),...  47.3 us
    unnamed x3, local copies, waits for them, and re-layouts  1.7 us

profile of v4, /device:TPU:4, one launch (start us, length us, event | category | flops | bytes accessed | tf_op | source)
XLA Modules:
  0.0 49.0 jit_solution(5319008054460444461)
XLA Ops:
  0.0 0.0 copy-start
  0.0 0.7 %copy-done = s32[512]{0:T(512)S(1)} copy-done((s32[512]{0:T(512)S(1)}, s32[512]{0:T(512)}, u32[]{:S(2)}) %copy-start) | copy-done | bytes 2072
  0.7 47.3 %shard_map.46 = f32[768,384]{1,0:T(8,128)S(1)} custom-call(f32[768,384]{1,0:T(8,128)} %mat_any.1, f32[8,768]{1,0:T(8,128)} %pan_any.1, f32[512,512]{1,0:T(8,128)} %inv_any.1, s32[1,512]{1,0:T(1,128)S(1)} %bitcast.1), custom_call_target="tpu_custom_call" | custom-call | tf_op jit(solution)/shard_map/pallas_call | solution.py:450
  48.0 1.0 %copy.6 = f32[768,384]{1,0:T(8,128)} copy(f32[768,384]{1,0:T(8,128)S(1)} %shard_map.46) | data formatting | bytes 2359296
Async XLA Ops:
  0.0 0.7 %copy-start = (s32[512]{0:T(512)S(1)}, s32[512]{0:T(512)}, u32[]{:S(2)}) copy-start(s32[512]{0:T(512)} %param.7) | copy-start | bytes 6148
